TPU v7x, 32 devices: a whole 2x2x4 slice. The times are simulated.
32 devices in a mesh: col: 16 (over z, x, core), row: 2 (over y).
Axes of the slice: x: 2, y: 2, z: 4, core: 2. Of those that a mesh axis runs over, the one named last changes fastest.
Arguments:
- matrix: float32 [2048, 2048], P('row', 'col'), as said below
- row_diag: float32 [2, 2048], P(None, 'row'), may hold values from 0.8 to 1.2
- col_diag: float32 [2, 2048], P(None, 'col'), may hold values from 0.8 to 1.2
Outputs:
- factored: float32 [2048, 2048], P('row', 'col')
Inputs may be any that keep to these rules, and one draw needn't show every extreme that they name: `matrix`: off the diagonal the entries lie within -6 and 6; the diagonal entries exceed 1.5 * sqrt(512) - 6.
All inputs are finite; a program needn't handle non-finite values.
Results may differ from a plain program's by a relative error of at most 0.0001.
Values sent between devices are 32-bit elements; how exact they have to be, the bound alone decides.
No kernel may reach another device: no remote copies, remote signals or barrier semaphores. Data moves between devices by JAX's collectives and lax.ppermute only.
A program may use at most 64 MiB of HBM per device.

v0:
```python
import jax
import jax.numpy as jnp
from jax import lax
from jax.sharding import PartitionSpec as P

PW = 256
PANELS = 2
inv_root = 0.7071067811865476


def swapped(x, axis, distance):
    return lax.ppermute(x, axis, [(i, i ^ 1 << distance) for i in range(lax.axis_size(axis))])


def from_root(x, axis, root):
    mine = lax.axis_index(axis) == root
    return lax.psum(jnp.where(mine, x, jnp.zeros_like(x)), axis)


def lu_block(block):
    size = block.shape[0]
    places = jnp.arange(size)

    def eliminate(step, current):
        pivot = current[step, step]
        below = places > step
        column = jnp.where(below, current[:, step] / pivot, 0.0)
        across = jnp.where(below, current[step, :], 0.0)
        current = current - column[:, None] * across[None, :]
        return jnp.where((places == step)[None, :] & below[:, None], column[:, None], current)

    return lax.fori_loop(0, size, eliminate, block)


def hdot(left, right):
    return jnp.dot(left, right, precision=lax.Precision.HIGHEST, preferred_element_type=jnp.float32)


def strict_inverse(strict):
    size = strict.shape[0]
    identity = jnp.eye(size, dtype=strict.dtype)
    result = identity - strict
    power = strict
    exponent = 1
    while exponent * 2 < size:
        power = hdot(power, power)
        exponent = exponent * 2
        result = hdot(result, identity + power)
    return result


def inverses(packed):
    upper_factor = jnp.triu(packed)
    lower_inverse = strict_inverse(jnp.tril(packed, -1))
    pivots = jnp.diagonal(packed)
    scaled = jnp.triu(packed, 1) / pivots[:, None]
    upper_inverse = strict_inverse(scaled) / pivots[None, :]
    return (lower_inverse, upper_inverse, upper_factor)


def pair_mix(own, partner, is_first, scales):
    return scales * jnp.where(is_first, own + partner, partner - own) * inv_root


def shards(matrix, row_diag, col_diag):
    height, width = matrix.shape
    row_pos = lax.axis_index("row")
    col_pos = lax.axis_index("col")
    first_row = row_pos * height
    first_col = col_pos * width
    rows = first_row + jnp.arange(height, dtype=jnp.int32)[:, None]
    cols = first_col + jnp.arange(width, dtype=jnp.int32)[None, :]
    partner = swapped(matrix, "row", 0)
    current = pair_mix(matrix, partner, row_pos == 0, row_diag[0][:, None])
    half = height // 2
    upper_part, lower_part = (current[:half], current[half:])
    current = jnp.concatenate(
        [
            row_diag[1][:half, None] * (upper_part + lower_part) * inv_root,
            row_diag[1][half:, None] * (upper_part - lower_part) * inv_root,
        ],
        0,
    )
    top_bit = lax.axis_size("col").bit_length() - 2
    partner = swapped(current, "col", top_bit)
    current = pair_mix(current, partner, col_pos // 2**top_bit % 2 == 0, col_diag[0][None, :])
    partner = swapped(current, "col", top_bit - 1)
    current = pair_mix(
        current, partner, col_pos // 2 ** (top_bit - 1) % 2 == 0, col_diag[1][None, :]
    )
    count = PW // width
    for panel in range(PANELS):
        start = panel * PW
        stop = start + PW
        owner = start // width
        offset = jnp.clip(start - first_row, 0, height - PW)
        band_local = lax.dynamic_slice_in_dim(current, offset, PW, 0)
        panel_parts = []
        for piece in range(count):
            panel_parts.append(from_root(current, "col", owner + piece))
        panel_block = jnp.concatenate(panel_parts, 1)
        diag_local = lax.dynamic_slice_in_dim(panel_block, offset, PW, 0)
        diag_block, band_rows = (from_root(diag_local, "row", 0), from_root(band_local, "row", 0))
        packed = lu_block(diag_block)
        lower_inverse, upper_inverse, upper_factor = inverses(packed)
        lower_rows = hdot(panel_block, upper_inverse)
        upper_cols = hdot(lower_inverse, band_rows)
        below = rows >= stop
        right = cols >= stop
        inside = (cols >= start) & (cols < stop)
        updated = current - hdot(
            jnp.where(below, lower_rows, 0.0), jnp.where(right, upper_cols, 0.0)
        )
        col_offset = jnp.clip(first_col - start, 0, PW - width)
        lower_cols = lax.dynamic_slice_in_dim(lower_rows, col_offset, width, 1)
        updated = jnp.where(below & inside, lower_cols, updated)
        packed_cols = lax.dynamic_slice_in_dim(packed, col_offset, width, 1)
        new_band = jnp.where(right, upper_cols, jnp.where(inside, packed_cols, band_rows))
        placed = lax.dynamic_update_slice_in_dim(updated, new_band, offset, 0)
        in_band = (rows >= start) & (rows < stop)
        current = jnp.where(in_band, placed, updated)
    return current


def solution(mesh):
    in_specs = (P("row", "col"), P(None, "row"), P(None, "col"))
    out_specs = P("row", "col")
    return jax.shard_map(shards, mesh=mesh, in_specs=in_specs, out_specs=out_specs, check_vma=False)
```

profile of v0, /device:TPU:0, one launch (start us, length us, event | category | flops | bytes accessed | tf_op | source)
XLA Modules:
  0.0 1171.0 jit_solution(15443678754477894416)
XLA Ops:
  6.5 3.0 collective-permute-start
  9.6 12.1 %collective-permute-done = f32[1024,128]{1,0:T(8,128)S(1)} collective-permute-done((f32[1024,128]{1,0:T(8,128)}, f32[1024,128]{1,0:T(8,128)S(1)}, u32[]{:S(2)}, u32[]{:S(2)}) %collective-permute-start) | collective-permute-done | bytes 524320 | tf_op jit(solution)/shard_map/ppermute | solution.py:12
  21.7 1.2 multiply_multiply_fusion.2
  23.2 2.9 collective-permute-start.1
  26.7 21.7 %collective-permute-done.1 = f32[1024,128]{1,0:T(8,128)S(1)} collective-permute-done((f32[1024,128]{1,0:T(8,128)S(1)}, f32[1024,128]{1,0:T(8,128)S(1)}, u32[]{:S(2)}, u32[]{:S(2)}) %collective-permute-start.1) | collective-permute-done | bytes 524320 | tf_op jit(solution)/shard_map/ppermute | solution.py:12
  49.2 12.3 %collective-permute-done.2 = f32[1024,128]{1,0:T(8,128)S(1)} collective-permute-done((f32[1024,128]{1,0:T(8,128)S(1)}, f32[1024,128]{1,0:T(8,128)S(1)}, u32[]{:S(2)}, u32[]{:S(2)}) %collective-permute-start.2) | collective-permute-done | bytes 524320 | tf_op jit(solution)/shard_map/ppermute | solution.py:12
  64.1 95.2 %all-reduce.11.cloned.1.call-done = (f32[1024,128]{1,0:T(8,128)}, f32[1024,128]{1,0:T(8,128)}) async-done(((f32[1024,128]{1,0:T(8,128)}, f32[1024,128]{1,0:T(8,128)}), (f32[1024,128]{1,0:T(8,128)}, f32[1024,128]{1,0:T(8,128)})) %all-reduce.11.cloned.1.call-update) | async-done | bytes 1048592 | tf_op jit(solution)/shard_map/psum | solution.py:17
  159.3 1.1 constant_dynamic-update-slice_fusion.1
  161.4 25.2 %all-reduce.15.cloned.1.call-done = (f32[256,256]{1,0:T(8,128)}, f32[256,128]{1,0:T(8,128)}) async-done(((f32[256,256]{1,0:T(8,128)}, f32[256,128]{1,0:T(8,128)}), (f32[256,256]{1,0:T(8,128)}, f32[256,128]{1,0:T(8,128)})) %all-reduce.15.cloned.1.call-update) | async-done | bytes 393232 | tf_op jit(solution)/shard_map/psum | solution.py:17
  186.7 1.1 copy.16
  187.7 407.8 %while.30 = (s32[]{:T(128)}, f32[256,256]{0,1:T(8,128)S(1)}, s32[]{:T(128)}) while((s32[]{:T(128)}, f32[256,256]{0,1:T(8,128)S(1)}, s32[]{:T(128)}) %tuple.81), condition=%wide.region_4.5_spmd.clone.clone, body=%wide.region_3.4_spmd.clone.clone.sunk | while | flops 263426 | bytes 1056337 | solution.py:32
  595.7 2.5 gather_fusion
  605.3 1.0 fusion.80
  611.5 1.0 fusion.4
  612.7 1.0 select_n.267
  613.7 1.1 broadcast_select_fusion
  615.5 93.4 %all-reduce.9.cloned.1.call-done = (f32[1024,128]{1,0:T(8,128)}, f32[1024,128]{1,0:T(8,128)}) async-done(((f32[1024,128]{1,0:T(8,128)}, f32[1024,128]{1,0:T(8,128)}), (f32[1024,128]{1,0:T(8,128)}, f32[1024,128]{1,0:T(8,128)})) %all-reduce.9.cloned.1.call-update) | async-done | bytes 1048592 | tf_op jit(solution)/shard_map/psum | solution.py:17
  708.9 1.1 constant_dynamic-update-slice_fusion.3
  711.0 25.1 %all-reduce.13.cloned.1.call-done = (f32[256,256]{1,0:T(8,128)}, f32[256,128]{1,0:T(8,128)}) async-done(((f32[256,256]{1,0:T(8,128)}, f32[256,128]{1,0:T(8,128)}), (f32[256,256]{1,0:T(8,128)}, f32[256,128]{1,0:T(8,128)})) %all-reduce.13.cloned.1.call-update) | async-done | bytes 393232 | tf_op jit(solution)/shard_map/psum | solution.py:17
  736.1 1.1 copy.20
  737.2 407.8 %while.31 = (s32[]{:T(128)}, f32[256,256]{0,1:T(8,128)S(1)}, s32[]{:T(128)}) while((s32[]{:T(128)}, f32[256,256]{0,1:T(8,128)S(1)}, s32[]{:T(128)}) %tuple.84), condition=%wide.region_10.11_spmd.clone.clone, body=%wide.region_9.10_spmd.clone.clone.sunk | while | flops 263426 | bytes 1056337 | solution.py:32
  1145.2 2.6 gather_fusion.1
  1161.0 1.0 fusion.5
  1162.8 1.7 select_n.284
  (3181 shorter events, 822.0 us)
Async XLA Ops:
  6.5 3.0 copy-start.5
  6.5 152.8 %all-reduce.11.cloned.1.call-start = ((), (), s32[]{:S(2)}) async-start(), calls=%async_computation.1 | async-start | bytes 2097152 | tf_op jit(solution)/shard_map/psum | solution.py:17
  6.5 15.1 %collective-permute-start = (f32[1024,128]{1,0:T(8,128)}, f32[1024,128]{1,0:T(8,128)S(1)}, u32[]{:S(2)}, u32[]{:S(2)}) collective-permute-start(f32[1024,128]{1,0:T(8,128)} %param.7), channel_id=1, source_target_pairs={{0,1},{1,0},{2,3},{3,2},{4,5},{5,4},{6,7},{7,6},{8,9},{9,8},{10,11... | collective-permute-start | bytes 1572872 | tf_op jit(solution)/shard_map/ppermute | solution.py:12
  9.5 12.1 %slice-start = ((f32[2,1024]{1,0:T(2,128)}), f32[1,1024]{1,0:T(1,128)S(1)}, s32[]{:S(2)}) async-start(f32[2,1024]{1,0:T(2,128)} %param.8), calls=%async_computation.4 | async-start | bytes 8192 | tf_op jit(solution)/shard_map/slice | solution.py:74
  23.2 25.3 %collective-permute-start.1 = (f32[1024,128]{1,0:T(8,128)S(1)}, f32[1024,128]{1,0:T(8,128)S(1)}, u32[]{:S(2)}, u32[]{:S(2)}) collective-permute-start(f32[1024,128]{1,0:T(8,128)S(1)} %pad_maximum_fusion), channel_id=1, source_target_pairs={{0,16},{2,18},{4,20},{6,22},{8,24},{10,26},{12,28},{14,30},{16,0},... | collective-permute-start | bytes 1572872 | tf_op jit(solution)/shard_map/ppermute | solution.py:12
  26.0 0.7 copy-start.6
  48.5 13.0 %collective-permute-start.2 = (f32[1024,128]{1,0:T(8,128)S(1)}, f32[1024,128]{1,0:T(8,128)S(1)}, u32[]{:S(2)}, u32[]{:S(2)}) collective-permute-start(f32[1024,128]{1,0:T(8,128)S(1)} %multiply_multiply_fusion.1), channel_id=1, source_target_pairs={{0,8},{2,10},{4,12},{6,14},{8,0},{10,2},{12,4},{14,6},{16,24},{18,... | collective-permute-start | bytes 1572872 | tf_op jit(solution)/shard_map/ppermute | solution.py:12
  63.3 123.4 %all-reduce.15.cloned.1.call-start = ((), (), s32[]{:S(2)}) async-start(), calls=%async_computation.3 | async-start | bytes 786432 | tf_op jit(solution)/shard_map/psum | solution.py:17
  159.3 1.2 copy-start.1
  161.3 547.6 %all-reduce.9.cloned.1.call-start = ((), (), s32[]{:S(2)}) async-start(), calls=%async_computation | async-start | bytes 2097152 | tf_op jit(solution)/shard_map/psum | solution.py:17
  610.2 0.9 copy-start.4
  614.8 121.3 %all-reduce.13.cloned.1.call-start = ((), (), s32[]{:S(2)}) async-start(), calls=%async_computation.2 | async-start | bytes 786432 | tf_op jit(solution)/shard_map/psum | solution.py:17
  708.9 1.2 copy-start.2
  1159.7 0.9 copy-start.3
  1162.0 0.8 copy-start
Sparse Core Ops, SparseCore 0:
  63.4 95.8 all-reduce.10
  161.7 24.8 all-reduce.14
  615.0 93.9 all-reduce.8
  711.2 24.8 all-reduce.12
where the time goes:
time: 1180 us; the launch traced here: 1170 us
  other arithmetic  427 us (36%)
  local copies, waits for them, and re-layouts  384 us (33%)
  waiting for transfers between devices  285 us (24%)
  matrix products  27 us (2%)
  loops' own time  26.7 us (2%)
  between operations  13.9 us (1%)
    select_n x512, other arithmetic, eliminate(): column = jnp.where(below, current[:, step] / pivot, 0.0)  335 us
    dynamic_slice x512, local copies, waits for them, and re-layouts, eliminate(): pivot = current[step, step]  303 us
    psum x4, waiting for transfers between devices, from_root(): return lax.psum(jnp.where(mine, x, jnp.zeros_like(x)), axis)  239 us
    select_n x512, other arithmetic, eliminate(): jnp.where((places == step)[None, :] & below[:, None], column[:, None], cu...  75.5 us
    while x512, local copies, waits for them, and re-layouts  65.8 us
    ppermute x3, waiting for transfers between devices, swapped(): lax.ppermute(x, axis, [(i, i ^ 1 << distance) for i in range(lax.axis_siz...  46.1 us
    dot_general x62, matrix products, hdot(): jnp.dot(left, right, precision=lax.Precision.HIGHEST, preferred_element_t...  27 us
    another operation x2, loops' own time, lu_block(): return lax.fori_loop(0, size, eliminate, block)  26.7 us
  transfers between devices with their start and end apart: 7, of which 7 were waited for; matrix products, arithmetic and copies ran while one was open for 0% of the time, Pallas kernels for 0%

commit v1 on v0

--- a/solution.py
+++ b/solution.py
@@ -14,7 +14,7 @@
 
 def from_root(x, axis, root):
     mine = lax.axis_index(axis) == root
-    return lax.psum(jnp.where(mine, x, jnp.zeros_like(x)), axis)
+    return jnp.sum(lax.all_gather(jnp.where(mine, x, jnp.zeros_like(x)), axis), axis=0)
 
 
 def lu_block(block):

time: 1180 us -> 1260 us (1.068)
  waiting for transfers between devices: 285 us -> 325 us
  blocking collectives: 0 us -> 29.7 us
  other arithmetic: 427 us -> 440 us
    all_gather x0 -> x4, waiting for transfers between devices: none -> 279 us  [from_root(): lax.all_gather(jnp.where(mine, x, jnp.zeros_like(x)), axis)]
    psum x4 -> x0, waiting for transfers between devices: 239 us -> none  [from_root(): return lax.psum(jnp.where(mine, x, jnp.zeros_like(x)), axis)]
    all_gather x0 -> x4, blocking collectives: none -> 29.7 us  [from_root(): lax.all_gather(jnp.where(mine, x, jnp.zeros_like(x)), axis)]
    reduce_sum x0 -> x8, other arithmetic: none -> 15.4 us  [from_root(): jnp.sum(lax.all_gather(jnp.where(mine, x, jnp.zeros_like(x)), axis), axis=0)]
  transfers between devices with their start and end apart: 7 -> 7, of which waited for: 7 -> 7; matrix products, arithmetic and copies ran while one was open for 0% -> 1% of each run, Pallas kernels for 0% -> 0%
where the time goes in v1:
time: 1260 us; the launch traced here: 1250 us
  other arithmetic  440 us (35%)
  local copies, waits for them, and re-layouts  380 us (30%)
  waiting for transfers between devices  325 us (26%)
  blocking collectives  29.7 us (2%)
  matrix products  27.1 us (2%)
  loops' own time  26.7 us (2%)
  between operations  13.9 us (1%)
    select_n x512, other arithmetic, eliminate(): column = jnp.where(below, current[:, step] / pivot, 0.0)  335 us
    dynamic_slice x512, local copies, waits for them, and re-layouts, eliminate(): pivot = current[step, step]  303 us
    all_gather x4, waiting for transfers between devices, from_root(): lax.all_gather(jnp.where(mine, x, jnp.zeros_like(x)), axis)  279 us
    select_n x512, other arithmetic, eliminate(): jnp.where((places == step)[None, :] & below[:, None], column[:, None], cu...  75.2 us
    while x512, local copies, waits for them, and re-layouts  65.8 us
    ppermute x3, waiting for transfers between devices, swapped(): lax.ppermute(x, axis, [(i, i ^ 1 << distance) for i in range(lax.axis_siz...  44.6 us
    all_gather x4, blocking collectives, from_root(): lax.all_gather(jnp.where(mine, x, jnp.zeros_like(x)), axis)  29.7 us
    dot_general x62, matrix products, hdot(): jnp.dot(left, right, precision=lax.Precision.HIGHEST, preferred_element_t...  27.1 us
  transfers between devices with their start and end apart: 7, of which 7 were waited for; matrix products, arithmetic and copies ran while one was open for 1% of the time, Pallas kernels for 0%

profile of v1, /device:TPU:0, one launch (start us, length us, event | category | flops | bytes accessed | tf_op | source)
XLA Modules:
  0.0 1248.5 jit_solution(6807263854618078027)
XLA Ops:
  6.5 3.0 collective-permute-start
  10.9 10.7 collective-permute-done
  21.7 1.2 multiply_multiply_fusion.2
  23.2 2.9 collective-permute-start.1
  26.8 21.7 %collective-permute-done.1 = f32[1024,128]{1,0:T(8,128)S(1)} collective-permute-done((f32[1024,128]{1,0:T(8,128)S(1)}, f32[1024,128]{1,0:T(8,128)S(1)}, u32[]{:S(2)}, u32[]{:S(2)}) %collective-permute-start.1) | collective-permute-done | bytes 524320 | tf_op jit(solution)/shard_map/ppermute | solution.py:12
  49.2 12.3 collective-permute-done.2
  64.3 5.6 all-gather.3
  69.9 69.8 %all-gather.13.cloned.1.call-done = f32[16384,128]{1,0:T(8,128)} async-done(((f32[1024,128]{1,0:T(8,128)}), f32[16384,128]{1,0:T(8,128)}) %all-gather.13.cloned.1.call-update) | async-done | bytes 8388624 | tf_op jit(solution)/shard_map/all_gather | solution.py:17
  139.7 3.8 reduce_sum.72
  143.6 71.2 %all-gather.15.cloned.1.call-done = f32[16384,128]{1,0:T(8,128)} async-done(((f32[1024,128]{1,0:T(8,128)}), f32[16384,128]{1,0:T(8,128)}) %all-gather.15.cloned.1.call-update) | async-done | bytes 8388624 | tf_op jit(solution)/shard_map/all_gather | solution.py:17
  214.8 3.8 reduce_sum.73
  218.7 9.1 all-gather.2
  228.0 407.7 %while.30 = (s32[]{:T(128)}, f32[256,256]{0,1:T(8,128)S(1)}, s32[]{:T(128)}) while((s32[]{:T(128)}, f32[256,256]{0,1:T(8,128)S(1)}, s32[]{:T(128)}) %tuple.79), condition=%wide.region_4.5_spmd.clone.clone, body=%wide.region_3.4_spmd.clone.clone.sunk | while | flops 263426 | bytes 1056329 | solution.py:32
  637.2 2.5 gather_fusion
  651.1 1.1 fusion.4
  655.0 5.9 all-gather.7
  660.9 66.5 %all-gather.17.cloned.1.call-done = f32[16384,128]{1,0:T(8,128)} async-done(((f32[1024,128]{1,0:T(8,128)}), f32[16384,128]{1,0:T(8,128)}) %all-gather.17.cloned.1.call-update) | async-done | bytes 8388624 | tf_op jit(solution)/shard_map/all_gather | solution.py:17
  727.4 3.8 reduce_sum.76
  731.3 71.1 %all-gather.19.cloned.1.call-done = f32[16384,128]{1,0:T(8,128)} async-done(((f32[1024,128]{1,0:T(8,128)}), f32[16384,128]{1,0:T(8,128)}) %all-gather.19.cloned.1.call-update) | async-done | bytes 8388624 | tf_op jit(solution)/shard_map/all_gather | solution.py:17
  802.3 3.8 reduce_sum.77
  806.2 9.1 all-gather.6
  815.5 407.7 %while.31 = (s32[]{:T(128)}, f32[256,256]{0,1:T(8,128)S(1)}, s32[]{:T(128)}) while((s32[]{:T(128)}, f32[256,256]{0,1:T(8,128)S(1)}, s32[]{:T(128)}) %tuple.82), condition=%wide.region_10.11_spmd.clone.clone, body=%wide.region_9.10_spmd.clone.clone.sunk | while | flops 263426 | bytes 1056329 | solution.py:32
  1224.7 2.4 gather_fusion.1
  1240.3 1.7 select_n.284
  (3176 shorter events, 824.9 us)
Async XLA Ops:
  6.5 133.2 %all-gather.13.cloned.1.call-start = ((), (), s32[]{:S(2)}) async-start(), calls=%async_computation | async-start | bytes 8912896 | tf_op jit(solution)/shard_map/all_gather | solution.py:17
  6.5 15.1 %collective-permute-start = (f32[1024,128]{1,0:T(8,128)}, f32[1024,128]{1,0:T(8,128)S(1)}, u32[]{:S(2)}, u32[]{:S(2)}) collective-permute-start(f32[1024,128]{1,0:T(8,128)} %param.7), channel_id=1, source_target_pairs={{0,1},{1,0},{2,3},{3,2},{4,5},{5,4},{6,7},{7,6},{8,9},{9,8},{10,11... | collective-permute-start | bytes 1572872 | tf_op jit(solution)/shard_map/ppermute | solution.py:12
  23.2 25.3 %collective-permute-start.1 = (f32[1024,128]{1,0:T(8,128)S(1)}, f32[1024,128]{1,0:T(8,128)S(1)}, u32[]{:S(2)}, u32[]{:S(2)}) collective-permute-start(f32[1024,128]{1,0:T(8,128)S(1)} %pad_maximum_fusion.4), channel_id=1, source_target_pairs={{0,16},{2,18},{4,20},{6,22},{8,24},{10,26},{12,28},{14,30},{16,0},... | collective-permute-start | bytes 1572872 | tf_op jit(solution)/shard_map/ppermute | solution.py:12
  48.5 13.0 %collective-permute-start.2 = (f32[1024,128]{1,0:T(8,128)S(1)}, f32[1024,128]{1,0:T(8,128)S(1)}, u32[]{:S(2)}, u32[]{:S(2)}) collective-permute-start(f32[1024,128]{1,0:T(8,128)S(1)} %multiply_multiply_fusion.1), channel_id=1, source_target_pairs={{0,8},{2,10},{4,12},{6,14},{8,0},{10,2},{12,4},{14,6},{16,24},{18,... | collective-permute-start | bytes 1572872 | tf_op jit(solution)/shard_map/ppermute | solution.py:12
  63.2 151.6 %all-gather.15.cloned.1.call-start = ((), (), s32[]{:S(2)}) async-start(), calls=%async_computation.1 | async-start | bytes 8912896 | tf_op jit(solution)/shard_map/all_gather | solution.py:17
  64.0 663.4 %all-gather.17.cloned.1.call-start = ((), (), s32[]{:S(2)}) async-start(), calls=%async_computation.2 | async-start | bytes 8912896 | tf_op jit(solution)/shard_map/all_gather | solution.py:17
  654.4 147.9 %all-gather.19.cloned.1.call-start = ((), (), s32[]{:S(2)}) async-start(), calls=%async_computation.3 | async-start | bytes 8912896 | tf_op jit(solution)/shard_map/all_gather | solution.py:17
  1239.5 0.8 copy-start
Sparse Core Ops, SparseCore 0:
  63.4 76.3 all-gather.12
  141.9 72.8 all-gather.14
  654.5 72.8 all-gather.16
  729.4 72.8 all-gather.18
